TPU v7x, 128 devices: a whole 4x4x4 slice. The times are simulated.
128 devices in a mesh: row: 16 (over x, z), col: 8 (over y, core).
Axes of the slice: x: 4, y: 4, z: 4, core: 2. Of those that a mesh axis runs over, the one named last changes fastest.
Arguments:
- t_upper: bfloat16 [3, 4096, 4096], P(None, 'row', 'col'), may hold values from -0.03125 to 0.03125
- t_old: bfloat16 [3, 4096, 24576], P(None, 'row', 'col'), may hold values from -0.03125 to 0.03125
- inverses: bfloat16 [3, 4096, 4096], P(None, 'row', 'col'), may hold values from -1 to 1.5, as said below
- forcing: float32 [3, 4096, 128], P(None, 'row'), may hold values from -6 to 6
- x_old: bfloat16 [24576, 128], P('col'), may hold values from -6 to 6
- offsets: float32 [128], replicated, may hold values from -0.5 to 0.5
- starts: int32 [128], replicated, may hold values from 0 to 36864
- column_map: int32 [128], replicated, may hold values from 0 to 127, each once
- z_cols: bfloat16 [49152, 3, 4096], P('row', None, 'col'), may hold values from -0.0546875 to 0.0546875
- acc: float32 [49152, 128], P(('row', 'col')), may hold values from -6 to 6
Outputs:
- solved: float32 [3, 4096, 128], P(None, ('row', 'col'))
- acc_out: float32 [49152, 128], P(('row', 'col'))
Inputs may be any that keep to these rules, and one draw needn't show every extreme that they name: `inverses`: dense matrices with a dominant positive diagonal.
All inputs are finite; a program needn't handle non-finite values.
Results may differ from a plain program's by a relative error of at most 0.0003.
Values may be sent and summed in bfloat16 or wider, within the bound.
No kernel may reach another device: no remote copies, remote signals or barrier semaphores. Data moves between devices by JAX's collectives and lax.ppermute only.
A program may use at most 128 MiB of HBM per device.

v0:
```python
import jax
import jax.numpy as jnp
from jax import lax
from jax.sharding import PartitionSpec as P

NEUMANN = 3


def split_pair(values):
    upper = values.astype(jnp.bfloat16)
    lower = (values - lax.optimization_barrier(upper).astype(jnp.float32)).astype(jnp.bfloat16)
    return jnp.concatenate([upper, lower], axis=-1)


def body(t_upper, t_old, inverses, forcing, x_old, offsets, starts, column_map, z_cols, acc):
    n_col = lax.axis_size("col")
    row_idx = lax.axis_index("row")
    col_idx = lax.axis_index("col")
    steps = forcing.shape[0]
    row_block = t_upper.shape[1]
    col_block = t_upper.shape[2]
    width = forcing.shape[2]
    old_cols = x_old.shape[0]
    full_rows = col_block * n_col
    share = row_block // n_col
    pairs = {}
    count = 0
    for first in range(steps):
        for second in range(first + 1, steps):
            pairs[first, second] = count
            count = count + 1

    def fold_pair(product):
        return product[:, :width] + product[:, width:]

    old_rows = steps * full_rows + col_idx * old_cols + jnp.arange(old_cols, dtype=jnp.int32)
    old_live = old_rows[:, None] < starts[None, :]
    old_vals = jnp.where(old_live, x_old, jnp.zeros_like(x_old))
    local_start = row_idx * row_block

    def reduce_rows(partial_value):
        return lax.psum(partial_value, "col")

    def spread_rows(values):
        return lax.all_gather(values, "row", axis=0, tiled=True)

    def own_cols(whole):
        return lax.dynamic_slice_in_dim(whole, col_idx * col_block, col_block, 0)

    solved_full = {}
    pieces = {}
    for step in reversed(range(steps)):
        partial_value = -jnp.dot(t_old[step], old_vals, preferred_element_type=jnp.float32)
        for later in range(step + 1, steps):
            partial_value = partial_value - fold_pair(
                jnp.dot(
                    t_upper[pairs[step, later]],
                    own_cols(solved_full[later]),
                    preferred_element_type=jnp.float32,
                )
            )
        rhs = reduce_rows(partial_value) + forcing[step]
        gathered = spread_rows(split_pair(rhs))
        term = reduce_rows(
            fold_pair(
                jnp.dot(inverses[step], own_cols(gathered), preferred_element_type=jnp.float32)
            )
        )
        total = term
        for extra in range(1, NEUMANN):
            gathered = spread_rows(split_pair(term))
            term = (
                reduce_rows(
                    fold_pair(
                        jnp.dot(
                            inverses[step], own_cols(gathered), preferred_element_type=jnp.float32
                        )
                    )
                )
                * offsets[None, :]
            )
            total = total + term
        rows = step * full_rows + local_start + jnp.arange(row_block, dtype=jnp.int32)
        total = jnp.where(rows[:, None] < starts[None, :], total, jnp.zeros_like(total))
        pieces[step] = lax.dynamic_slice_in_dim(total, col_idx * share, share, 0)
        solved_full[step] = spread_rows(split_pair(total))
    stacked = jnp.concatenate([own_cols(solved_full[step]) for step in range(steps)], axis=0)
    one_hot = (jnp.arange(width, dtype=jnp.int32)[:, None] == column_map[None, :]).astype(
        jnp.bfloat16
    )
    picked_upper = jnp.dot(stacked[:, :width], one_hot, preferred_element_type=jnp.float32).astype(
        jnp.bfloat16
    )
    picked_lower = jnp.dot(stacked[:, width:], one_hot, preferred_element_type=jnp.float32).astype(
        jnp.bfloat16
    )
    picked = jnp.concatenate([picked_upper, picked_lower], axis=1)
    z_rows = z_cols.shape[0]
    z_flat = z_cols.reshape(z_rows, steps * col_block)
    contribution = lax.psum_scatter(
        fold_pair(jnp.dot(z_flat, picked, preferred_element_type=jnp.float32)),
        "col",
        scatter_dimension=0,
        tiled=True,
    )
    solved = jnp.stack([pieces[step] for step in range(steps)])
    return (solved, acc + contribution)


def solution(mesh):
    placed = (
        P(None, "row", "col"),
        P(None, "row", "col"),
        P(None, "row", "col"),
        P(None, "row", None),
        P("col", None),
        P(),
        P(),
        P(),
        P("row", None, "col"),
        P(("row", "col"), None),
    )
    return jax.shard_map(
        body,
        mesh=mesh,
        in_specs=placed,
        out_specs=(P(None, ("row", "col"), None), P(("row", "col"), None)),
        check_vma=False,
    )
```

profile of v0, /device:TPU:0, one launch (start us, length us, event | category | flops | bytes accessed | tf_op | source)
XLA Modules:
  0.0 1396.4 jit_solution(2241294068387488249)
XLA Ops:
  11.0 62.4 %all-reduce.13.cloned.1.call-done = f32[256,128]{0,1:T(8,128)} async-done(((f32[256,128]{0,1:T(8,128)}), f32[256,128]{0,1:T(8,128)}) %all-reduce.13.cloned.1.call-update) | async-done | bytes 131088 | tf_op jit(solution)/shard_map/psum | solution.py:42
  76.0 46.2 %all-gather.13.cloned.1.call-done = bf16[4096,256]{0,1:T(8,128)(2,1)} async-done(((bf16[256,256]{0,1:T(8,128)(2,1)}), bf16[4096,256]{0,1:T(8,128)(2,1)}) %all-gather.13.cloned.1.call-update) | async-done | bytes 2097168 | tf_op jit(solution)/shard_map/all_gather | solution.py:45
  124.2 60.2 %all-reduce.15.cloned.1.call-done = f32[256,128]{0,1:T(8,128)} async-done(((f32[256,128]{0,1:T(8,128)}), f32[256,128]{0,1:T(8,128)}) %all-reduce.15.cloned.1.call-update) | async-done | bytes 131088 | tf_op jit(solution)/shard_map/psum | solution.py:42
  187.0 46.2 %all-gather.15.cloned.1.call-done = bf16[4096,256]{0,1:T(8,128)(2,1)} async-done(((bf16[256,256]{0,1:T(8,128)(2,1)}), bf16[4096,256]{0,1:T(8,128)(2,1)}) %all-gather.15.cloned.1.call-update) | async-done | bytes 2097168 | tf_op jit(solution)/shard_map/all_gather | solution.py:45
  235.2 60.1 %all-reduce.17.cloned.1.call-done = f32[256,128]{0,1:T(8,128)} async-done(((f32[256,128]{0,1:T(8,128)}), f32[256,128]{0,1:T(8,128)}) %all-reduce.17.cloned.1.call-update) | async-done | bytes 131088 | tf_op jit(solution)/shard_map/psum | solution.py:42
  298.1 46.2 %all-gather.17.cloned.1.call-done = bf16[4096,256]{0,1:T(8,128)(2,1)} async-done(((bf16[256,256]{0,1:T(8,128)(2,1)}), bf16[4096,256]{0,1:T(8,128)(2,1)}) %all-gather.17.cloned.1.call-update) | async-done | bytes 2097168 | tf_op jit(solution)/shard_map/all_gather | solution.py:45
  346.3 60.2 %all-reduce.19.cloned.1.call-done = f32[256,128]{0,1:T(8,128)} async-done(((f32[256,128]{0,1:T(8,128)}), f32[256,128]{0,1:T(8,128)}) %all-reduce.19.cloned.1.call-update) | async-done | bytes 131088 | tf_op jit(solution)/shard_map/psum | solution.py:42
  408.3 47.0 %all-gather.19.cloned.1.call-done = bf16[4096,256]{0,1:T(8,128)(2,1)} async-done(((bf16[256,256]{0,1:T(8,128)(2,1)}), bf16[4096,256]{0,1:T(8,128)(2,1)}) %all-gather.19.cloned.1.call-update) | async-done | bytes 2097168 | tf_op jit(solution)/shard_map/all_gather | solution.py:45
  460.3 59.3 %all-reduce.21.cloned.1.call-done = f32[256,128]{0,1:T(8,128)} async-done(((f32[256,128]{0,1:T(8,128)}), f32[256,128]{0,1:T(8,128)}) %all-reduce.21.cloned.1.call-update) | async-done | bytes 131088 | tf_op jit(solution)/shard_map/psum | solution.py:42
  522.1 46.2 %all-gather.21.cloned.1.call-done = bf16[4096,256]{0,1:T(8,128)(2,1)} async-done(((bf16[256,256]{0,1:T(8,128)(2,1)}), bf16[4096,256]{0,1:T(8,128)(2,1)}) %all-gather.21.cloned.1.call-update) | async-done | bytes 2097168 | tf_op jit(solution)/shard_map/all_gather | solution.py:45
  570.3 60.2 %all-reduce.23.cloned.1.call-done = f32[256,128]{0,1:T(8,128)} async-done(((f32[256,128]{0,1:T(8,128)}), f32[256,128]{0,1:T(8,128)}) %all-reduce.23.cloned.1.call-update) | async-done | bytes 131088 | tf_op jit(solution)/shard_map/psum | solution.py:42
  633.2 46.2 %all-gather.23.cloned.1.call-done = bf16[4096,256]{0,1:T(8,128)(2,1)} async-done(((bf16[256,256]{0,1:T(8,128)(2,1)}), bf16[4096,256]{0,1:T(8,128)(2,1)}) %all-gather.23.cloned.1.call-update) | async-done | bytes 2097168 | tf_op jit(solution)/shard_map/all_gather | solution.py:45
  681.4 60.2 %all-reduce.25.cloned.1.call-done = f32[256,128]{0,1:T(8,128)} async-done(((f32[256,128]{0,1:T(8,128)}), f32[256,128]{0,1:T(8,128)}) %all-reduce.25.cloned.1.call-update) | async-done | bytes 131088 | tf_op jit(solution)/shard_map/psum | solution.py:42
  744.4 46.2 %all-gather.25.cloned.1.call-done = bf16[4096,256]{0,1:T(8,128)(2,1)} async-done(((bf16[256,256]{0,1:T(8,128)(2,1)}), bf16[4096,256]{0,1:T(8,128)(2,1)}) %all-gather.25.cloned.1.call-update) | async-done | bytes 2097168 | tf_op jit(solution)/shard_map/all_gather | solution.py:45
  792.6 60.1 %all-reduce.27.cloned.1.call-done = f32[256,128]{0,1:T(8,128)} async-done(((f32[256,128]{0,1:T(8,128)}), f32[256,128]{0,1:T(8,128)}) %all-reduce.27.cloned.1.call-update) | async-done | bytes 131088 | tf_op jit(solution)/shard_map/psum | solution.py:42
  854.7 46.6 %all-gather.27.cloned.1.call-done = bf16[4096,256]{0,1:T(8,128)(2,1)} async-done(((bf16[256,256]{0,1:T(8,128)(2,1)}), bf16[4096,256]{0,1:T(8,128)(2,1)}) %all-gather.27.cloned.1.call-update) | async-done | bytes 2097168 | tf_op jit(solution)/shard_map/all_gather | solution.py:45
  906.3 59.3 %all-reduce.29.cloned.1.call-done = f32[256,128]{0,1:T(8,128)} async-done(((f32[256,128]{0,1:T(8,128)}), f32[256,128]{0,1:T(8,128)}) %all-reduce.29.cloned.1.call-update) | async-done | bytes 131088 | tf_op jit(solution)/shard_map/psum | solution.py:42
  968.1 46.2 %all-gather.29.cloned.1.call-done = bf16[4096,256]{0,1:T(8,128)(2,1)} async-done(((bf16[256,256]{0,1:T(8,128)(2,1)}), bf16[4096,256]{0,1:T(8,128)(2,1)}) %all-gather.29.cloned.1.call-update) | async-done | bytes 2097168 | tf_op jit(solution)/shard_map/all_gather | solution.py:45
  1016.3 60.2 %all-reduce.31.cloned.1.call-done = f32[256,128]{0,1:T(8,128)} async-done(((f32[256,128]{0,1:T(8,128)}), f32[256,128]{0,1:T(8,128)}) %all-reduce.31.cloned.1.call-update) | async-done | bytes 131088 | tf_op jit(solution)/shard_map/psum | solution.py:42
  1079.2 46.2 %all-gather.31.cloned.1.call-done = bf16[4096,256]{0,1:T(8,128)(2,1)} async-done(((bf16[256,256]{0,1:T(8,128)(2,1)}), bf16[4096,256]{0,1:T(8,128)(2,1)}) %all-gather.31.cloned.1.call-update) | async-done | bytes 2097168 | tf_op jit(solution)/shard_map/all_gather | solution.py:45
  1127.3 60.2 %all-reduce.33.cloned.1.call-done = f32[256,128]{0,1:T(8,128)} async-done(((f32[256,128]{0,1:T(8,128)}), f32[256,128]{0,1:T(8,128)}) %all-reduce.33.cloned.1.call-update) | async-done | bytes 131088 | tf_op jit(solution)/shard_map/psum | solution.py:42
  1190.4 46.2 %all-gather.33.cloned.1.call-done = bf16[4096,256]{0,1:T(8,128)(2,1)} async-done(((bf16[256,256]{0,1:T(8,128)(2,1)}), bf16[4096,256]{0,1:T(8,128)(2,1)}) %all-gather.33.cloned.1.call-update) | async-done | bytes 2097168 | tf_op jit(solution)/shard_map/all_gather | solution.py:45
  1238.6 60.2 %all-reduce.35.cloned.1.call-done = f32[256,128]{0,1:T(8,128)} async-done(((f32[256,128]{0,1:T(8,128)}), f32[256,128]{0,1:T(8,128)}) %all-reduce.35.cloned.1.call-update) | async-done | bytes 131088 | tf_op jit(solution)/shard_map/psum | solution.py:42
  1313.2 34.3 %all-gather.35.cloned.1.call-done = bf16[4096,256]{0,1:T(8,128)(2,1)} async-done(((bf16[256,256]{0,1:T(8,128)(2,1)}), bf16[4096,256]{0,1:T(8,128)(2,1)}) %all-gather.35.cloned.1.call-update) | async-done | bytes 2097168 | tf_op jit(solution)/shard_map/all_gather | solution.py:45
  (164 shorter events, 115.4 us)
Async XLA Ops:
  10.8 111.4 %all-gather.13.cloned.1.call-start = ((), (), s32[]{:S(2)}) async-start(), calls=%async_computation.2 | async-start | bytes 2228224 | tf_op jit(solution)/shard_map/all_gather | solution.py:45
  75.9 108.5 %all-reduce.15.cloned.1.call-start = ((), (), s32[]{:S(2)}) async-start(), calls=%async_computation.3 | async-start | bytes 262144 | tf_op jit(solution)/shard_map/psum | solution.py:42
  124.1 109.1 %all-gather.15.cloned.1.call-start = ((), (), s32[]{:S(2)}) async-start(), calls=%async_computation.4 | async-start | bytes 2228224 | tf_op jit(solution)/shard_map/all_gather | solution.py:45
  187.0 108.3 %all-reduce.17.cloned.1.call-start = ((), (), s32[]{:S(2)}) async-start(), calls=%async_computation.5 | async-start | bytes 262144 | tf_op jit(solution)/shard_map/psum | solution.py:42
  235.2 109.1 %all-gather.17.cloned.1.call-start = ((), (), s32[]{:S(2)}) async-start(), calls=%async_computation.6 | async-start | bytes 2228224 | tf_op jit(solution)/shard_map/all_gather | solution.py:45
  298.1 108.4 %all-reduce.19.cloned.1.call-start = ((), (), s32[]{:S(2)}) async-start(), calls=%async_computation.7 | async-start | bytes 262144 | tf_op jit(solution)/shard_map/psum | solution.py:42
  346.2 109.1 %all-gather.19.cloned.1.call-start = ((), (), s32[]{:S(2)}) async-start(), calls=%async_computation.8 | async-start | bytes 2228224 | tf_op jit(solution)/shard_map/all_gather | solution.py:45
  408.2 111.3 %all-reduce.21.cloned.1.call-start = ((), (), s32[]{:S(2)}) async-start(), calls=%async_computation.9 | async-start | bytes 262144 | tf_op jit(solution)/shard_map/psum | solution.py:42
  460.1 108.2 %all-gather.21.cloned.1.call-start = ((), (), s32[]{:S(2)}) async-start(), calls=%async_computation.10 | async-start | bytes 2228224 | tf_op jit(solution)/shard_map/all_gather | solution.py:45
  522.1 108.5 %all-reduce.23.cloned.1.call-start = ((), (), s32[]{:S(2)}) async-start(), calls=%async_computation.11 | async-start | bytes 262144 | tf_op jit(solution)/shard_map/psum | solution.py:42
  570.3 109.1 %all-gather.23.cloned.1.call-start = ((), (), s32[]{:S(2)}) async-start(), calls=%async_computation.12 | async-start | bytes 2228224 | tf_op jit(solution)/shard_map/all_gather | solution.py:45
  633.1 108.4 %all-reduce.25.cloned.1.call-start = ((), (), s32[]{:S(2)}) async-start(), calls=%async_computation.13 | async-start | bytes 262144 | tf_op jit(solution)/shard_map/psum | solution.py:42
  681.3 109.3 %all-gather.25.cloned.1.call-start = ((), (), s32[]{:S(2)}) async-start(), calls=%async_computation.14 | async-start | bytes 2228224 | tf_op jit(solution)/shard_map/all_gather | solution.py:45
  744.3 108.3 %all-reduce.27.cloned.1.call-start = ((), (), s32[]{:S(2)}) async-start(), calls=%async_computation.15 | async-start | bytes 262144 | tf_op jit(solution)/shard_map/psum | solution.py:42
  792.5 108.8 %all-gather.27.cloned.1.call-start = ((), (), s32[]{:S(2)}) async-start(), calls=%async_computation.16 | async-start | bytes 2228224 | tf_op jit(solution)/shard_map/all_gather | solution.py:45
  854.4 111.2 %all-reduce.29.cloned.1.call-start = ((), (), s32[]{:S(2)}) async-start(), calls=%async_computation.17 | async-start | bytes 262144 | tf_op jit(solution)/shard_map/psum | solution.py:42
  906.1 108.2 %all-gather.29.cloned.1.call-start = ((), (), s32[]{:S(2)}) async-start(), calls=%async_computation.18 | async-start | bytes 2228224 | tf_op jit(solution)/shard_map/all_gather | solution.py:45
  968.1 108.4 %all-reduce.31.cloned.1.call-start = ((), (), s32[]{:S(2)}) async-start(), calls=%async_computation.19 | async-start | bytes 262144 | tf_op jit(solution)/shard_map/psum | solution.py:42
  1016.2 109.1 %all-gather.31.cloned.1.call-start = ((), (), s32[]{:S(2)}) async-start(), calls=%async_computation.20 | async-start | bytes 2228224 | tf_op jit(solution)/shard_map/all_gather | solution.py:45
  1079.1 108.5 %all-reduce.33.cloned.1.call-start = ((), (), s32[]{:S(2)}) async-start(), calls=%async_computation.21 | async-start | bytes 262144 | tf_op jit(solution)/shard_map/psum | solution.py:42
  1127.3 109.3 %all-gather.33.cloned.1.call-start = ((), (), s32[]{:S(2)}) async-start(), calls=%async_computation.22 | async-start | bytes 2228224 | tf_op jit(solution)/shard_map/all_gather | solution.py:45
  1190.3 108.5 %all-reduce.35.cloned.1.call-start = ((), (), s32[]{:S(2)}) async-start(), calls=%async_computation.23 | async-start | bytes 262144 | tf_op jit(solution)/shard_map/psum | solution.py:42
  1238.5 109.0 %all-gather.35.cloned.1.call-start = ((), (), s32[]{:S(2)}) async-start(), calls=%async_computation.24 | async-start | bytes 2228224 | tf_op jit(solution)/shard_map/all_gather | solution.py:45
  1300.5 87.6 %reduce-scatter.2.cloned.1.call-start = ((), (), s32[]{:S(2)}) async-start(), calls=%async_computation.25 | async-start | bytes 1769472 | tf_op jit(solution)/shard_map/reduce_scatter | solution.py:100
  (14 other events, 1878.5 us)
Sparse Core Ops, SparseCore 0:
  11.0 62.3 all-reduce.12
  76.1 46.0 all-gather.12
  125.1 59.2 all-reduce.14
  187.1 46.0 all-gather.14
  236.0 59.2 all-reduce.16
  298.2 46.0 all-gather.16
  347.2 59.2 all-reduce.18
  409.2 46.0 all-gather.18
  460.2 59.2 all-reduce.20
  522.2 46.0 all-gather.20
  571.2 59.2 all-reduce.22
  633.3 46.0 all-gather.22
  682.3 59.2 all-reduce.24
  744.4 46.0 all-gather.24
  793.3 59.2 all-reduce.26
  855.2 46.0 all-gather.26
  906.2 59.2 all-reduce.28
  968.2 46.0 all-gather.28
  1017.2 59.2 all-reduce.30
  1079.2 46.0 all-gather.30
  1128.3 59.2 all-reduce.32
  1190.4 46.0 all-gather.32
  1239.5 59.2 all-reduce.34
  1301.3 46.0 all-gather.34
  (1 shorter events, 32.2 us)
where the time goes:
time: 1400 us
  waiting for transfers between devices  1300 us (93%)
  other arithmetic  37.5 us (3%)
  matrix products  28.1 us (2%)
  local copies, waits for them, and re-layouts  17.3 us (1%)
  between operations  14.6 us (1%)
    psum x12, waiting for transfers between devices, reduce_rows(): return lax.psum(partial_value, 'col')  723 us
    all_gather x12, waiting for transfers between devices, spread_rows(): return lax.all_gather(values, 'row', axis=0, tiled=True)  544 us
    reduce_scatter x1, waiting for transfers between devices, body(): lax.psum_scatter(fold_pair(jnp.dot(z_flat, picked, preferred_element_type...  31.1 us
  transfers between devices with their start and end apart: 25, of which 25 were waited for; matrix products, arithmetic and copies ran while one was open for 1% of the time, Pallas kernels for 0%

commit v1 on v0

--- a/solution.py
+++ b/solution.py
@@ -42,7 +42,9 @@
         return lax.psum(partial_value, "col")
 
     def spread_rows(values):
-        return lax.all_gather(values, "row", axis=0, tiled=True)
+        return jnp.concatenate(
+            lax.all_to_all(jnp.stack([values] * lax.axis_size("row")), "row", 0, 0), axis=0
+        )
 
     def own_cols(whole):
         return lax.dynamic_slice_in_dim(whole, col_idx * col_block, col_block, 0)

time: 1400 us -> 1230 us (0.88)
  waiting for transfers between devices: 1300 us -> 867 us
  blocking collectives: 0 us -> 230 us
  starting transfers between devices: 1.04 us -> 35.7 us
    all_gather x12 -> x0, waiting for transfers between devices: 544 us -> none  [spread_rows(): return lax.all_gather(values, 'row', axis=0, tiled=True)]
    all_to_all x0 -> x7, blocking collectives: none -> 230 us  [spread_rows(): lax.all_to_all(jnp.stack([values] * lax.axis_size('row')), 'row', 0, 0)]
    all_to_all x0 -> x5, waiting for transfers between devices: none -> 124 us  [spread_rows(): lax.all_to_all(jnp.stack([values] * lax.axis_size('row')), 'row', 0, 0)]
    all_to_all x0 -> x5, starting transfers between devices: none -> 35.1 us  [spread_rows(): lax.all_to_all(jnp.stack([values] * lax.axis_size('row')), 'row', 0, 0)]
  transfers between devices with their start and end apart: 25 -> 18, of which waited for: 25 -> 18; matrix products, arithmetic and copies ran while one was open for 1% -> 1% of each run, Pallas kernels for 0% -> 0%
where the time goes in v1:
time: 1230 us
  waiting for transfers between devices  867 us (70%)
  blocking collectives  230 us (19%)
  starting transfers between devices  35.7 us (3%)
  other arithmetic  29.2 us (2%)
  local copies, waits for them, and re-layouts  26.5 us (2%)
  matrix products  23.5 us (2%)
  between operations  14.6 us (1%)
    psum x12, waiting for transfers between devices, reduce_rows(): return lax.psum(partial_value, 'col')  711 us
    all_to_all x7, blocking collectives, spread_rows(): lax.all_to_all(jnp.stack([values] * lax.axis_size('row')), 'row', 0, 0)  230 us
    all_to_all x5, waiting for transfers between devices, spread_rows(): lax.all_to_all(jnp.stack([values] * lax.axis_size('row')), 'row', 0, 0)  124 us
    all_to_all x5, starting transfers between devices, spread_rows(): lax.all_to_all(jnp.stack([values] * lax.axis_size('row')), 'row', 0, 0)  35.1 us
    reduce_scatter x1, waiting for transfers between devices, body(): lax.psum_scatter(fold_pair(jnp.dot(z_flat, picked, preferred_element_type...  31.6 us
  transfers between devices with their start and end apart: 18, of which 18 were waited for; matrix products, arithmetic and copies ran while one was open for 1% of the time, Pallas kernels for 0%

profile of v1, /device:TPU:0, one launch (start us, length us, event | category | flops | bytes accessed | tf_op | source)
XLA Modules:
  0.0 1227.1 jit_solution(8008030036907660119)
XLA Ops:
  11.6 61.9 %all-reduce.13.cloned.1.call-done = f32[256,128]{0,1:T(8,128)} async-done(((f32[256,128]{0,1:T(8,128)}), f32[256,128]{0,1:T(8,128)}) %all-reduce.13.cloned.1.call-update) | async-done | bytes 131088 | tf_op jit(solution)/shard_map/psum | solution.py:42
  84.1 27.7 %all-to-all-done = bf16[16,256,256]{2,1,0:T(8,128)(2,1)S(1)} async-done(((bf16[16,256,256]{2,1,0:T(8,128)(2,1)}), bf16[16,256,256]{2,1,0:T(8,128)(2,1)S(1)}, u32[]{:S(2)}, u32[]{:S(2)}) %all-to-all-start) | async-done | bytes 2097184 | tf_op jit(solution)/shard_map/all_to_all | solution.py:46
  112.9 60.2 %all-reduce.15.cloned.1.call-done = f32[256,128]{0,1:T(8,128)} async-done(((f32[256,128]{0,1:T(8,128)}), f32[256,128]{0,1:T(8,128)}) %all-reduce.15.cloned.1.call-update) | async-done | bytes 131088 | tf_op jit(solution)/shard_map/psum | solution.py:42
  175.3 32.9 %all_to_all.60 = bf16[16,256,256]{2,1,0:T(8,128)(2,1)S(1)} all-to-all(bf16[16,256,256]{2,1,0:T(8,128)(2,1)S(1)} %stack.33), channel_id=1, replica_groups=mesh['row'=16,'col'=8] {'row'}, dimensions={0} | all-to-all | bytes 4194304 | tf_op jit(solution)/shard_map/all_to_all | solution.py:46
  209.1 58.5 %all-reduce.17.cloned.1.call-done = f32[256,128]{0,1:T(8,128)} async-done(((f32[256,128]{0,1:T(8,128)}), f32[256,128]{0,1:T(8,128)}) %all-reduce.17.cloned.1.call-update) | async-done | bytes 131088 | tf_op jit(solution)/shard_map/psum | solution.py:42
  278.4 27.7 %all-to-all-done.2 = bf16[16,256,256]{2,1,0:T(8,128)(2,1)S(1)} async-done(((bf16[16,256,256]{2,1,0:T(8,128)(2,1)}), bf16[16,256,256]{2,1,0:T(8,128)(2,1)S(1)}, u32[]{:S(2)}, u32[]{:S(2)}) %all-to-all-start.2) | async-done | bytes 2097184 | tf_op jit(solution)/shard_map/all_to_all | solution.py:46
  307.1 60.2 %all-reduce.19.cloned.1.call-done = f32[256,128]{0,1:T(8,128)} async-done(((f32[256,128]{0,1:T(8,128)}), f32[256,128]{0,1:T(8,128)}) %all-reduce.19.cloned.1.call-update) | async-done | bytes 131088 | tf_op jit(solution)/shard_map/psum | solution.py:42
  368.7 33.0 %all_to_all.61 = bf16[16,256,256]{2,1,0:T(8,128)(2,1)S(1)} all-to-all(bf16[16,256,256]{2,1,0:T(8,128)(2,1)S(1)} %stack.35), channel_id=1, replica_groups=mesh['row'=16,'col'=8] {'row'}, dimensions={0} | all-to-all | bytes 4194304 | tf_op jit(solution)/shard_map/all_to_all | solution.py:46
  406.9 58.3 %all-reduce.21.cloned.1.call-done = f32[256,128]{0,1:T(8,128)} async-done(((f32[256,128]{0,1:T(8,128)}), f32[256,128]{0,1:T(8,128)}) %all-reduce.21.cloned.1.call-update) | async-done | bytes 131088 | tf_op jit(solution)/shard_map/psum | solution.py:42
  467.3 32.9 %all_to_all.62 = bf16[16,256,256]{2,1,0:T(8,128)(2,1)S(1)} all-to-all(bf16[16,256,256]{2,1,0:T(8,128)(2,1)S(1)} %stack.36), channel_id=1, replica_groups=mesh['row'=16,'col'=8] {'row'}, dimensions={0} | all-to-all | bytes 4194304 | tf_op jit(solution)/shard_map/all_to_all | solution.py:46
  501.2 58.4 %all-reduce.23.cloned.1.call-done = f32[256,128]{0,1:T(8,128)} async-done(((f32[256,128]{0,1:T(8,128)}), f32[256,128]{0,1:T(8,128)}) %all-reduce.23.cloned.1.call-update) | async-done | bytes 131088 | tf_op jit(solution)/shard_map/psum | solution.py:42
  561.8 32.9 %all_to_all.63 = bf16[16,256,256]{2,1,0:T(8,128)(2,1)S(1)} all-to-all(bf16[16,256,256]{2,1,0:T(8,128)(2,1)S(1)} %stack.37), channel_id=1, replica_groups=mesh['row'=16,'col'=8] {'row'}, dimensions={0} | all-to-all | bytes 4194304 | tf_op jit(solution)/shard_map/all_to_all | solution.py:46
  595.7 58.5 %all-reduce.25.cloned.1.call-done = f32[256,128]{0,1:T(8,128)} async-done(((f32[256,128]{0,1:T(8,128)}), f32[256,128]{0,1:T(8,128)}) %all-reduce.25.cloned.1.call-update) | async-done | bytes 131088 | tf_op jit(solution)/shard_map/psum | solution.py:42
  664.9 27.7 %all-to-all-done.6 = bf16[16,256,256]{2,1,0:T(8,128)(2,1)S(1)} async-done(((bf16[16,256,256]{2,1,0:T(8,128)(2,1)}), bf16[16,256,256]{2,1,0:T(8,128)(2,1)S(1)}, u32[]{:S(2)}, u32[]{:S(2)}) %all-to-all-start.6) | async-done | bytes 2097184 | tf_op jit(solution)/shard_map/all_to_all | solution.py:46
  693.6 60.2 %all-reduce.27.cloned.1.call-done = f32[256,128]{0,1:T(8,128)} async-done(((f32[256,128]{0,1:T(8,128)}), f32[256,128]{0,1:T(8,128)}) %all-reduce.27.cloned.1.call-update) | async-done | bytes 131088 | tf_op jit(solution)/shard_map/psum | solution.py:42
  766.2 25.8 %all-to-all-done.7 = bf16[16,256,256]{2,1,0:T(8,128)(2,1)S(1)} async-done(((bf16[16,256,256]{2,1,0:T(8,128)(2,1)}), bf16[16,256,256]{2,1,0:T(8,128)(2,1)S(1)}, u32[]{:S(2)}, u32[]{:S(2)}) %all-to-all-start.7) | async-done | bytes 2097184 | tf_op jit(solution)/shard_map/all_to_all | solution.py:46
  797.0 60.1 %all-reduce.29.cloned.1.call-done = f32[256,128]{0,1:T(8,128)} async-done(((f32[256,128]{0,1:T(8,128)}), f32[256,128]{0,1:T(8,128)}) %all-reduce.29.cloned.1.call-update) | async-done | bytes 131088 | tf_op jit(solution)/shard_map/psum | solution.py:42
  859.3 32.9 %all_to_all.64 = bf16[16,256,256]{2,1,0:T(8,128)(2,1)S(1)} all-to-all(bf16[16,256,256]{2,1,0:T(8,128)(2,1)S(1)} %stack.40), channel_id=1, replica_groups=mesh['row'=16,'col'=8] {'row'}, dimensions={0} | all-to-all | bytes 4194304 | tf_op jit(solution)/shard_map/all_to_all | solution.py:46
  893.2 58.4 %all-reduce.31.cloned.1.call-done = f32[256,128]{0,1:T(8,128)} async-done(((f32[256,128]{0,1:T(8,128)}), f32[256,128]{0,1:T(8,128)}) %all-reduce.31.cloned.1.call-update) | async-done | bytes 131088 | tf_op jit(solution)/shard_map/psum | solution.py:42
  953.7 32.9 %all_to_all.65 = bf16[16,256,256]{2,1,0:T(8,128)(2,1)S(1)} all-to-all(bf16[16,256,256]{2,1,0:T(8,128)(2,1)S(1)} %stack.41), channel_id=1, replica_groups=mesh['row'=16,'col'=8] {'row'}, dimensions={0} | all-to-all | bytes 4194304 | tf_op jit(solution)/shard_map/all_to_all | solution.py:46
  987.6 58.4 %all-reduce.33.cloned.1.call-done = f32[256,128]{0,1:T(8,128)} async-done(((f32[256,128]{0,1:T(8,128)}), f32[256,128]{0,1:T(8,128)}) %all-reduce.33.cloned.1.call-update) | async-done | bytes 131088 | tf_op jit(solution)/shard_map/psum | solution.py:42
  1048.4 33.0 %all_to_all.66 = bf16[16,256,256]{2,1,0:T(8,128)(2,1)S(1)} all-to-all(bf16[16,256,256]{2,1,0:T(8,128)(2,1)S(1)} %stack.42), channel_id=1, replica_groups=mesh['row'=16,'col'=8] {'row'}, dimensions={0} | all-to-all | bytes 4194304 | tf_op jit(solution)/shard_map/all_to_all | solution.py:46
  1082.4 58.4 %all-reduce.35.cloned.1.call-done = f32[256,128]{0,1:T(8,128)} async-done(((f32[256,128]{0,1:T(8,128)}), f32[256,128]{0,1:T(8,128)}) %all-reduce.35.cloned.1.call-update) | async-done | bytes 131088 | tf_op jit(solution)/shard_map/psum | solution.py:42
  1187.2 31.6 %reduce-scatter.2.cloned.1.call-done = f32[384,128]{0,1:T(8,128)} async-done(((f32[3072,128]{0,1:T(8,128)}), f32[384,128]{0,1:T(8,128)}) %reduce-scatter.2.cloned.1.call-update) | async-done | bytes 196624 | tf_op jit(solution)/shard_map/reduce_scatter | solution.py:102
  (180 shorter events, 130.1 us)
Async XLA Ops:
  7.2 66.3 %all-reduce.13.cloned.1.call-start = ((), (), s32[]{:S(2)}) async-start(), calls=%async_computation.13 | async-start | bytes 262144 | tf_op jit(solution)/shard_map/psum | solution.py:42
  77.0 34.9 %all-to-all-start = ((bf16[16,256,256]{2,1,0:T(8,128)(2,1)}), bf16[16,256,256]{2,1,0:T(8,128)(2,1)S(1)}, u32[]{:S(2)}, u32[]{:S(2)}) async-start(bf16[16,256,256]{2,1,0:T(8,128)(2,1)} %stack.32), calls=%async_computation | async-start | bytes 4194304 | tf_op jit(solution)/shard_map/all_to_all | solution.py:46
  84.1 89.0 %all-reduce.15.cloned.1.call-start = ((), (), s32[]{:S(2)}) async-start(), calls=%async_computation.14 | async-start | bytes 262144 | tf_op jit(solution)/shard_map/psum | solution.py:42
  112.9 154.7 %all-reduce.17.cloned.1.call-start = ((), (), s32[]{:S(2)}) async-start(), calls=%async_computation.15 | async-start | bytes 262144 | tf_op jit(solution)/shard_map/psum | solution.py:42
  271.2 96.1 %copy-start.1 = (f32[256,128]{0,1:T(8,128)S(1)}, f32[256,128]{0,1:T(8,128)}, u32[]{:S(2)}) copy-start(f32[256,128]{0,1:T(8,128)} %all-reduce.15.cloned.1.call-done) | copy-start | bytes 393220
  271.2 96.1 %copy-start.4 = (f32[256,128]{0,1:T(8,128)S(1)}, f32[256,128]{0,1:T(8,128)}, u32[]{:S(2)}) copy-start(f32[256,128]{0,1:T(8,128)} %all-reduce.17.cloned.1.call-done) | copy-start | bytes 393220
  271.2 96.1 %copy-start.15 = (s32[128]{0:T(128)S(1)}, s32[128]{0:T(128)}, u32[]{:S(2)}) copy-start(s32[128]{0:T(128)} %param.16) | copy-start | bytes 1540
  271.2 34.9 %all-to-all-start.2 = ((bf16[16,256,256]{2,1,0:T(8,128)(2,1)}), bf16[16,256,256]{2,1,0:T(8,128)(2,1)S(1)}, u32[]{:S(2)}, u32[]{:S(2)}) async-start(bf16[16,256,256]{2,1,0:T(8,128)(2,1)} %stack.34), calls=%async_computation.2 | async-start | bytes 4194304 | tf_op jit(solution)/shard_map/all_to_all | solution.py:46
  278.3 89.0 %all-reduce.19.cloned.1.call-start = ((), (), s32[]{:S(2)}) async-start(), calls=%async_computation.16 | async-start | bytes 262144 | tf_op jit(solution)/shard_map/psum | solution.py:42
  307.1 158.1 %all-reduce.21.cloned.1.call-start = ((), (), s32[]{:S(2)}) async-start(), calls=%async_computation.17 | async-start | bytes 262144 | tf_op jit(solution)/shard_map/psum | solution.py:42
  406.7 152.9 %all-reduce.23.cloned.1.call-start = ((), (), s32[]{:S(2)}) async-start(), calls=%async_computation.18 | async-start | bytes 262144 | tf_op jit(solution)/shard_map/psum | solution.py:42
  501.2 152.9 %all-reduce.25.cloned.1.call-start = ((), (), s32[]{:S(2)}) async-start(), calls=%async_computation.19 | async-start | bytes 262144 | tf_op jit(solution)/shard_map/psum | solution.py:42
  657.8 96.1 %copy-start.2 = (f32[256,128]{0,1:T(8,128)S(1)}, f32[256,128]{0,1:T(8,128)}, u32[]{:S(2)}) copy-start(f32[256,128]{0,1:T(8,128)} %all-reduce.23.cloned.1.call-done) | copy-start | bytes 393220
  657.8 96.1 %copy-start.5 = (f32[256,128]{0,1:T(8,128)S(1)}, f32[256,128]{0,1:T(8,128)}, u32[]{:S(2)}) copy-start(f32[256,128]{0,1:T(8,128)} %all-reduce.25.cloned.1.call-done) | copy-start | bytes 393220
  657.8 34.9 %all-to-all-start.6 = ((bf16[16,256,256]{2,1,0:T(8,128)(2,1)}), bf16[16,256,256]{2,1,0:T(8,128)(2,1)S(1)}, u32[]{:S(2)}, u32[]{:S(2)}) async-start(bf16[16,256,256]{2,1,0:T(8,128)(2,1)} %stack.38), calls=%async_computation.6 | async-start | bytes 4194304 | tf_op jit(solution)/shard_map/all_to_all | solution.py:46
  664.9 89.0 %all-reduce.27.cloned.1.call-start = ((), (), s32[]{:S(2)}) async-start(), calls=%async_computation.20 | async-start | bytes 262144 | tf_op jit(solution)/shard_map/psum | solution.py:42
  757.2 34.7 %all-to-all-start.7 = ((bf16[16,256,256]{2,1,0:T(8,128)(2,1)}), bf16[16,256,256]{2,1,0:T(8,128)(2,1)S(1)}, u32[]{:S(2)}, u32[]{:S(2)}) async-start(bf16[16,256,256]{2,1,0:T(8,128)(2,1)} %stack.39), calls=%async_computation.7 | async-start | bytes 4194304 | tf_op jit(solution)/shard_map/all_to_all | solution.py:46
  764.2 92.9 %all-reduce.29.cloned.1.call-start = ((), (), s32[]{:S(2)}) async-start(), calls=%async_computation.21 | async-start | bytes 262144 | tf_op jit(solution)/shard_map/psum | solution.py:42
  796.9 154.7 %all-reduce.31.cloned.1.call-start = ((), (), s32[]{:S(2)}) async-start(), calls=%async_computation.22 | async-start | bytes 262144 | tf_op jit(solution)/shard_map/psum | solution.py:42
  893.1 152.9 %all-reduce.33.cloned.1.call-start = ((), (), s32[]{:S(2)}) async-start(), calls=%async_computation.23 | async-start | bytes 262144 | tf_op jit(solution)/shard_map/psum | solution.py:42
  987.6 153.2 %all-reduce.35.cloned.1.call-start = ((), (), s32[]{:S(2)}) async-start(), calls=%async_computation.24 | async-start | bytes 262144 | tf_op jit(solution)/shard_map/psum | solution.py:42
  1048.4 92.5 %copy-start.3 = (f32[256,128]{0,1:T(8,128)S(1)}, f32[256,128]{0,1:T(8,128)}, u32[]{:S(2)}) copy-start(f32[256,128]{0,1:T(8,128)} %all-reduce.31.cloned.1.call-done) | copy-start | bytes 393220
  1143.5 34.7 %all-to-all-start.11 = ((bf16[16,256,256]{2,1,0:T(8,128)(2,1)}), bf16[16,256,256]{2,1,0:T(8,128)(2,1)S(1)}, u32[]{:S(2)}, u32[]{:S(2)}) async-start(bf16[16,256,256]{2,1,0:T(8,128)(2,1)} %stack.47), calls=%async_computation.11 | async-start | bytes 4194304 | tf_op jit(solution)/shard_map/all_to_all | solution.py:46
  1150.5 68.3 %reduce-scatter.2.cloned.1.call-start = ((), (), s32[]{:S(2)}) async-start(), calls=%async_computation.25 | async-start | bytes 1769472 | tf_op jit(solution)/shard_map/reduce_scatter | solution.py:102
  (13 other events, 375.1 us)
Sparse Core Ops, SparseCore 0:
  10.9 62.4 all-reduce.12
  113.0 60.0 all-reduce.14
  209.2 58.2 all-reduce.16
  307.2 60.0 all-reduce.18
  406.8 58.2 all-reduce.20
  501.3 58.2 all-reduce.22
  595.8 58.2 all-reduce.24
  693.7 60.0 all-reduce.26
  797.0 60.0 all-reduce.28
  893.2 58.2 all-reduce.30
  987.7 58.2 all-reduce.32
  1082.5 58.2 all-reduce.34
  1185.6 33.1 reduce-scatter.1
